TPU v7x, 128 devices: a whole 4x4x4 slice. The times are simulated.
128 devices in a mesh: row: 2 (over core), col: 2 (over x_lo), depth: 32 (over z, y, x_hi).
Axes of the slice: x: 4 (x_hi: 2, x_lo: 2; x = x_hi * 2 + x_lo), y: 4, z: 4, core: 2. Of those that a mesh axis runs over, the one named last changes fastest.
Arguments:
- left_blocks: bfloat16 [32, 2, 32, 2, 128, 128], P('col', 'row', 'depth'), may hold values from -0.625 to 0.625
- left_cols: int32 [32, 2, 32, 2], replicated, may hold values from 0 to 7, as said below
- right_blocks: bfloat16 [512, 2, 2, 128, 128], P(('col', 'depth'), 'row'), may hold values from -0.625 to 0.625
- right_cols: int32 [512, 2, 2], replicated, may hold values from 0 to 3, as said below
Outputs:
- product: float32 [4096, 1024], P(('col', 'depth'), 'row')
Inputs may be any that keep to these rules, and one draw needn't show every extreme that they name: `left_cols`: within each group of 2 entries along the last dimension the values are distinct. `right_cols`: within each group of 2 entries along the last dimension the values are distinct.
All inputs are finite; a program needn't handle non-finite values.
Results may differ from a plain program's by a relative error of at most 0.0003.
Values may be sent and summed in bfloat16 or wider, within the bound.
A program may use at most 64 MiB of HBM per device.

v0:
```python
import jax
import jax.numpy as jnp
from jax import lax
from jax.sharding import PartitionSpec as P

BLK = 128
JB = 4


def from_root(value, axis, source):
    kept = jnp.where(lax.axis_index(axis) == source, value, 0).astype(value.dtype)
    return lax.psum(kept, axis)


def shifted(value, axis, by):
    devices = lax.axis_size(axis)
    return lax.ppermute(value, axis, [(i, (i + by) % devices) for i in range(devices)])


def local(left_blocks, left_cols, right_blocks, right_cols):
    sections = lax.axis_size("col")
    layers = lax.axis_size("depth")
    col_index = lax.axis_index("col")
    row_index = lax.axis_index("row")
    layer_index = lax.axis_index("depth")
    rows_here = left_blocks.shape[0]
    per_row = left_blocks.shape[1]
    kblock = right_blocks.shape[0]
    own_left = left_blocks[:, :, 0]
    own_right = right_blocks[:, 0]
    row_cols = lax.dynamic_slice_in_dim(left_cols, col_index * rows_here, rows_here, 0)
    layer_cols = lax.dynamic_index_in_dim(row_cols, layer_index, axis=2, keepdims=False)
    group_cols = lax.dynamic_index_in_dim(right_cols, row_index, axis=1, keepdims=False)
    levels = jnp.arange(JB, dtype=jnp.int32)

    def multiply(totals, left_panel, right_tile, group):
        a_cols = lax.dynamic_index_in_dim(layer_cols, group, axis=1, keepdims=False)
        first_row = (group * layers + layer_index) * kblock
        b_cols = lax.dynamic_slice_in_dim(group_cols, first_row, kblock, 0)
        chooser = (b_cols[:, :, None] == levels).astype(jnp.bfloat16)
        spread = jnp.einsum(
            "kbl,kbyz->klyz", chooser, right_tile, preferred_element_type=jnp.float32
        ).astype(jnp.bfloat16)
        picked = jnp.take(spread, a_cols, axis=0)
        return totals + jnp.einsum(
            "iaxy,ialyz->ixlz", left_panel, picked, preferred_element_type=jnp.float32
        )

    totals = jnp.zeros((rows_here, BLK, JB, BLK), jnp.float32)

    def panel_for(group):
        root_row = group // per_row
        slot_index = group % per_row
        own_panel = lax.dynamic_index_in_dim(own_left, slot_index, axis=1, keepdims=False)
        return from_root(own_panel, "row", root_row)

    def advance(section_num, carry):
        running, right_tile = carry
        group = (col_index + section_num) % sections
        next_tile = shifted(right_tile, "col", -1)
        running = multiply(running, panel_for(group), right_tile, group)
        return (running, next_tile)

    totals, right_tile = lax.fori_loop(0, sections - 1, advance, (totals, own_right))
    final_group = (col_index + sections - 1) % sections
    totals = multiply(totals, panel_for(final_group), right_tile, final_group)
    flat_totals = totals.reshape(rows_here * BLK, JB * BLK)
    reduced = lax.psum_scatter(flat_totals, "depth", scatter_dimension=0, tiled=True)
    return reduced


def solution(mesh):
    return jax.shard_map(
        local,
        mesh=mesh,
        in_specs=(
            P("col", "row", "depth", None, None, None),
            P(),
            P(("col", "depth"), "row", None, None, None),
            P(),
        ),
        out_specs=P(("col", "depth"), "row"),
        check_vma=False,
    )
```

profile of v0, /device:TPU:0, one launch (start us, length us, event | category | flops | bytes accessed | tf_op | source)
XLA Modules:
  0.0 256.1 jit_solution(10548839379261007974)
XLA Ops:
  6.5 0.0 copy-start.2
  6.5 0.0 copy-start.3
  6.5 0.0 all-reduce.3.cloned.1.call-start
  6.5 2.7 %fusion.8 = (bf16[16,2,128,128]{3,2,1,0:T(8,128)(2,1)}, bf16[16,2,128,128]{3,2,1,0:T(8,128)(2,1)}) fusion(bf16[16,1,1,2,128,128]{5,4,3,2,1,0:T(8,128)(2,1)} %param.6, pred[]{:T(512)S(6)} %eq.51, pred[]{:T(512)S(6)} %eq.56), kind=kLoop, calls=%fused_computation.18 | loop fusion | flops 1048576 | bytes 3145730 | tf_op jit(solution)/shard_map/while/body/eval_jaxpr/jit(_where)/select_n | solution.py:11
  9.3 0.0 all-reduce.3.cloned.1.call-update
  9.3 0.0 reduce-scatter.4.cloned.1.call-start
  9.4 0.0 copy-done.2
  9.4 0.5 copy.69
  9.9 1.7 collective-permute-start
  11.6 0.0 copy-done.3
  11.6 0.1 constant_dynamic-slice_fusion.1
  11.7 0.1 copy.34
  11.8 0.1 copy.41
  11.9 0.8 dynamic-slice_bitcast_fusion.1
  12.7 0.1 copy.43
  12.8 0.1 copy.44
  12.9 0.1 reshape.51
  12.9 0.1 copy.42
  13.0 0.1 copy.36
  13.1 0.1 copy.38
  13.2 0.1 reshape.47
  13.3 0.1 copy.35
  13.4 1.2 convolution_convert_fusion.1
  14.6 5.7 %gather_fusion = bf16[32,4,128,128]{3,1,2,0:T(4,128)(2,1)} fusion(bf16[8,4,128,128]{3,1,2,0:T(4,128)(2,1)S(1)} %convolution_convert_fusion.1, s32[1024]{0:T(1024)S(1)} %pad_clamp_fusion.1), kind=kCustom, calls=%fused_computation.clone | custom fusion | bytes 8388736 | tf_op jit(solution)/shard_map/while/body/eval_jaxpr/jit(_take)/gather | solution.py:44
  20.4 3.1 %collective-permute-done = bf16[8,2,128,128]{3,1,2,0:T(2,128)(2,1)S(1)} collective-permute-done((bf16[8,2,128,128]{3,1,2,0:T(2,128)(2,1)S(1)}, bf16[8,2,128,128]{3,1,2,0:T(2,128)(2,1)S(1)}, u32[]{:S(2)}, u32[]{:S(2)}) %collective-permute-start) | collective-permute-done | bytes 524320 | tf_op jit(solution)/shard_map/while/body/eval_jaxpr/ppermute | solution.py:17
  23.5 1.2 convolution_convert_fusion
  24.7 5.8 %gather_fusion.1 = bf16[32,4,128,128]{3,1,2,0:T(4,128)(2,1)} fusion(bf16[8,4,128,128]{3,1,2,0:T(4,128)(2,1)S(1)} %convolution_convert_fusion, s32[1024]{0:T(1024)S(1)} %pad_clamp_fusion), kind=kCustom, calls=%fused_computation.1.clone | custom fusion | bytes 8388736 | tf_op jit(solution)/shard_map/jit(_take)/gather | solution.py:44
  30.5 8.7 %all-reduce.3.cloned.1.call-done = (bf16[16,2,128,128]{3,2,1,0:T(8,128)(2,1)}, bf16[16,2,128,128]{3,2,1,0:T(8,128)(2,1)}) async-done(((bf16[16,2,128,128]{3,2,1,0:T(8,128)(2,1)}, bf16[16,2,128,128]{3,2,1,0:T(8,128)(2,1)}), (bf16[16,2,128,128]{3,2,1,0:T(8,128)(2,1)}, bf16[16,2,128,128]{3,2,1,0:T(8,128)(2,1)})) %all-reduce.3.cloned.1.call-update) | async-done | bytes 2097168 | tf_op jit(solution)/shard_map/psum | solution.py:12
  39.2 0.0 copy-start
  39.2 0.0 copy-start.1
  39.2 3.6 %fusion = f32[16,128,4,128,1]{3,1,4,2,0:T(8,128)S(1)} fusion(bf16[16,2,4,128,128]{4,2,3,1,0:T(4,128)(2,1)} %bitcast.66, pred[16,2]{1,0:T(8,128)(4,1)S(1)} %copy.42, bf16[16,2,128,128]{3,2,1,0:T(8,128)(2,1)} %get-tuple-element.24), kind=kOutput, calls=%fused_computation.5 | convolution fusion | flops 538968064 | bytes 9437216 | tf_op jit(solution)/shard_map/iaxy,ialyz->ixlz/dot_general | solution.py:45
  42.8 0.1 copy-done
  42.9 0.3 copy-done.1
  43.2 1.3 bitcast_add_fusion
  44.6 2.8 %copy.56 = f32[16,128,4,128]{3,2,1,0:T(4,128)S(1)} copy(f32[16,128,4,128]{3,1,2,0:T(8,128)S(1)} %bitcast_add_fusion) | data formatting | bytes 8388608
  47.4 2.4 copy.68
  49.8 0.0 reduce-scatter.4.cloned.1.call-update
  49.8 199.5 %reduce-scatter.4.cloned.1.call-done = f32[64,512]{1,0:T(8,128)} async-done(((f32[2048,512]{1,0:T(8,128)}), f32[64,512]{1,0:T(8,128)}) %reduce-scatter.4.cloned.1.call-update) | async-done | bytes 131088 | tf_op jit(solution)/shard_map/reduce_scatter | solution.py:68
  (5 shorter events, 0.0 us)
Async XLA Ops:
  6.5 2.8 %copy-start.2 = (bf16[8,1,2,128,128]{4,3,2,1,0:T(8,128)(2,1)S(1)}, bf16[8,1,2,128,128]{4,3,2,1,0:T(8,128)(2,1)}, u32[]{:S(2)}) copy-start(bf16[8,1,2,128,128]{4,3,2,1,0:T(8,128)(2,1)} %param.8) | copy-start | bytes 1572868
  6.5 5.0 %copy-start.3 = (s32[32,2,32,2]{2,3,1,0:T(2,128)S(1)}, s32[32,2,32,2]{2,3,1,0:T(2,128)}, u32[]{:S(2)}) copy-start(s32[32,2,32,2]{2,3,1,0:T(2,128)} %param.7) | copy-start | bytes 49156
  6.5 32.6 %all-reduce.3.cloned.1.call-start = ((), (), s32[]{:S(2)}) async-start(), calls=%async_computation.2 | async-start | bytes 4194304 | tf_op jit(solution)/shard_map/psum | solution.py:12
  9.3 240.0 %reduce-scatter.4.cloned.1.call-start = ((), (), s32[]{:S(2)}) async-start(), calls=%async_computation.1 | async-start | bytes 4325376 | tf_op jit(solution)/shard_map/reduce_scatter | solution.py:68
  9.9 13.6 %collective-permute-start = (bf16[8,2,128,128]{3,1,2,0:T(2,128)(2,1)S(1)}, bf16[8,2,128,128]{3,1,2,0:T(2,128)(2,1)S(1)}, u32[]{:S(2)}, u32[]{:S(2)}) collective-permute-start(bf16[8,2,128,128]{3,1,2,0:T(2,128)(2,1)S(1)} %bitcast.67), channel_id=1, source_target_pairs={{0,32},{32,0},{1,33},{33,1},{2,34},{34,2},{3,35},{35,3},{4,36},{36... | collective-permute-start | bytes 1572872 | tf_op jit(solution)/shard_map/while/body/eval_jaxpr/ppermute | solution.py:17
  39.2 3.7 %copy-start = (bf16[32,4,128,128]{3,1,2,0:T(4,128)(2,1)S(1)}, bf16[32,4,128,128]{3,1,2,0:T(4,128)(2,1)}, u32[]{:S(2)}) copy-start(bf16[32,4,128,128]{3,1,2,0:T(4,128)(2,1)} %gather_fusion) | copy-start | bytes 12582916
  39.2 4.0 %copy-start.1 = (bf16[16,2,128,128]{3,2,1,0:T(8,128)(2,1)S(1)}, bf16[16,2,128,128]{3,2,1,0:T(8,128)(2,1)}, u32[]{:S(2)}) copy-start(bf16[16,2,128,128]{3,2,1,0:T(8,128)(2,1)} %get-tuple-element.25) | copy-start | bytes 3145732
Sparse Core Ops, SparseCore 0:
  9.8 29.2 all-reduce.2
  49.9 199.3 reduce-scatter.3
where the time goes:
time: 256 us
  waiting for transfers between devices  211 us (82%)
  local copies, waits for them, and re-layouts  19.4 us (8%)
  between operations  13.5 us (5%)
  matrix products  7.41 us (3%)
  other arithmetic  2.79 us (1%)
    reduce_scatter x1, waiting for transfers between devices, local(): lax.psum_scatter(flat_totals, 'depth', scatter_dimension=0, tiled=True)  199 us
    gather x2, local copies, waits for them, and re-layouts, multiply(): picked = jnp.take(spread, a_cols, axis=0)  11.5 us
    psum x1, waiting for transfers between devices, from_root(): return lax.psum(kept, axis)  8.69 us
    unnamed x11, local copies, waits for them, and re-layouts  6.14 us
  transfers between devices with their start and end apart: 3, of which 3 were waited for; matrix products, arithmetic and copies ran while one was open for 6% of the time, Pallas kernels for 0%

commit v1 on v0

v1 whole, which is shorter than its diff:
```python
import jax
import jax.numpy as jnp
from jax import lax
from jax.experimental import pallas as pl
from jax.experimental.pallas import tpu as pltpu
from jax.sharding import PartitionSpec as P

BLK = 128
JB = 4
PASSES = 2
WIDTH = BLK // PASSES
NCOL = JB * WIDTH
ROWS = 16
KPG = 8
HALF = BLK // 2
TOP = 32767.0
MESH = pl.DeviceIdType.MESH


def coded(x, axes):
    peak = jnp.maximum(jnp.max(jnp.abs(x), axis=axes, keepdims=True), 1e-33)
    whole = jnp.round(x * (TOP / peak)).astype(jnp.int32).astype(jnp.int16)
    return whole, peak.reshape(1, NCOL) * (1.0 / TOP)


def decoded(whole, scale):
    return whole.astype(jnp.int32).astype(jnp.float32) * scale


def kernel(idx, left_hbm, right, out, left, packed, other, spread, acc, ubuf,
           q1s, q1r, s1s, s1r, q2s, q2r, s2s, s2r, q3s, q3r, s3s, s3r,
           lsem, xs, xr, a1s, a1r, b1s, b1r, a2s, a2r, b2s, b2r, a3s, a3r, b3s, b3r):
    r = lax.axis_index("row")
    c = lax.axis_index("col")
    d = lax.axis_index("depth")
    z, y, h = d // 8, (d // 2) % 4, d % 2

    def at(zz, yy, hh):
        return (r, c, (zz % 4) * 8 + (yy % 4) * 2 + hh)

    mate, peer, far = (1 - r, c, d), (r, 1 - c, d), at(z, y, 1 - h)
    along = (
        lambda by: at(z + by, y, h),
        lambda by: at(z, y + by, h),
    )
    barrier = pltpu.get_barrier_semaphore()
    peers = [mate, peer, far] + [go(by) for go in along for by in (1, 2, 3)]
    for device in peers:
        pl.semaphore_signal(barrier, inc=1, device_id=device, device_id_type=MESH)

    started = []

    def send(src, dst, ssem, rsem, device):
        copy = pltpu.make_async_remote_copy(
            src_ref=src, dst_ref=dst, send_sem=ssem, recv_sem=rsem,
            device_id=device, device_id_type=MESH)
        copy.start()
        started.append(copy)

    def arrived(src, dst, ssem, rsem):
        pltpu.make_async_remote_copy(
            src_ref=src, dst_ref=dst, send_sem=ssem, recv_sem=rsem,
            device_id=mate, device_id_type=MESH).wait_recv()

    mine = pltpu.make_async_copy(left_hbm, left.at[0], lsem)
    mine.start()

    low = lax.broadcasted_iota(jnp.int32, (BLK, BLK), 1) < HALF

    for k in range(KPG):
        one, two = right[k, 0], right[k, 1]
        packed[0, k] = jnp.concatenate([one[:, :HALF], two[:, :HALF]], axis=1)
        packed[1, k] = jnp.concatenate([one[:, HALF:], two[:, HALF:]], axis=1)

    pl.semaphore_wait(barrier, len(peers))
    for s in range(PASSES):
        send(packed.at[s], other.at[s], xs.at[s], xr.at[s], peer)
    send(left_hbm, left.at[1], xs.at[2], xr.at[2], mate)

    lane = lax.broadcasted_iota(jnp.int32, (1, BLK), 1)
    upper = (lane >= HALF).astype(jnp.int32)

    def widen(block, group, k):
        base = ROWS * 4 + (group * KPG + k) * 2
        j0, j1 = idx[base], idx[base + 1]
        turned = pltpu.roll(block, HALF, 1)
        straight = jnp.where(upper == 0, j0, j1)
        crossed = jnp.where(upper == 0, j1, j0)
        for t in range(2):
            target = upper + 2 * t
            keep = (straight == target).astype(jnp.float32).astype(jnp.bfloat16)
            swap = (crossed == target).astype(jnp.float32).astype(jnp.bfloat16)
            spread[group * KPG + k, :, t * BLK:(t + 1) * BLK] = block * keep + turned * swap

    def multiply(s):
        @pl.loop(0, ROWS // 4)
        def _(block_z):
            for block_y in range(4):
                i = block_z * 4 + block_y
                total = None
                for slot, group in ((0, r), (1, 1 - r)):
                    base = (i * 2 + group) * 2
                    a0, a1 = idx[base], idx[base + 1]
                    lhs = jnp.concatenate([left[slot, i, 0], left[slot, i, 1]], axis=1)
                    rhs = jnp.concatenate([spread[group * KPG + a0], spread[group * KPG + a1]], axis=0)
                    term = jnp.dot(lhs, rhs, preferred_element_type=jnp.float32)
                    total = term if total is None else total + term
                acc[s, block_z, block_y] = total

    where = (z, y)

    def own(s, part, pair, dest):
        if part == 0:
            return acc[s, dest, 2 * pair:2 * pair + 2, :HALF, :]
        return acc[s, 2 * pair:2 * pair + 2, dest, HALF:, :]

    def one(s, part, w, dest):
        if part == 0:
            return acc[s, dest, w, :HALF, :]
        return acc[s, w, dest, HALF:, :]

    def post1(s, part, slot, value, by):
        whole, scale = coded(value, (0, 1))
        q1s[s, part, slot] = whole
        s1s[s, part, slot] = scale
        n = (s * 2 + part) * 6 + slot
        send(q1s.at[s, part, slot], q1r.at[s, part, slot], a1s.at[n], a1r.at[n], along[part](by))
        send(s1s.at[s, part, slot], s1r.at[s, part, slot], b1s.at[n], b1r.at[n], along[part](by))

    def got1(s, part, slot):
        n = (s * 2 + part) * 6 + slot
        arrived(q1s.at[s, part, slot], q1r.at[s, part, slot], a1s.at[n], a1r.at[n])
        arrived(s1s.at[s, part, slot], s1r.at[s, part, slot], b1s.at[n], b1r.at[n])

    def stage1_open(s):
        for part in range(2):
            v = where[part]
            post1(s, part, 0, own(s, part, 0, (v + 2) % 4), 1)
            post1(s, part, 1, own(s, part, 1, (v + 2) % 4), 3)
        for part in range(2):
            v = where[part]
            post1(s, part, 3, own(s, part, 1, (v + 1) % 4), 1)
            post1(s, part, 4, own(s, part, 0, (v + 3) % 4), 3)

    def stage1_relay(s):
        for part in range(2):
            v = where[part]
            for slot, pair, by in ((0, 0, 1), (1, 1, 3)):
                got1(s, part, slot)
                value = own(s, part, pair, (v + by) % 4) + decoded(q1r[s, part, slot], s1r[s, part, slot])
                post1(s, part, 2 if slot == 0 else 5, value, by)

    def reduced(s, part, w):
        value = one(s, part, w, where[part])
        for first in (2, 4):
            pair = first + w // 2
            value = value + decoded(q1r[s, part, pair, w % 2], s1r[s, part, pair])
        return value

    def stage2(s):
        for part in range(2):
            for slot in (3, 4, 2, 5):
                got1(s, part, slot)
            v = where[1 - part]
            for by in (2, 1, 3):
                whole, scale = coded(reduced(s, part, (v + by) % 4), 0)
                q2s[s, part, by - 1] = whole
                s2s[s, part, by - 1] = scale
                n = (s * 2 + part) * 3 + by - 1
                send(q2s.at[s, part, by - 1], q2r.at[s, part, by - 1], a2s.at[n], a2r.at[n], along[1 - part](by))
                send(s2s.at[s, part, by - 1], s2r.at[s, part, by - 1], b2s.at[n], b2r.at[n], along[1 - part](by))
            ubuf[s, part] = reduced(s, part, v)

    def stage3(s):
        for part in range(2):
            value = ubuf[s, part]
            for by in range(3):
                n = (s * 2 + part) * 3 + by
                arrived(q2s.at[s, part, by], q2r.at[s, part, by], a2s.at[n], a2r.at[n])
                arrived(s2s.at[s, part, by], s2r.at[s, part, by], b2s.at[n], b2r.at[n])
                value = value + decoded(q2r[s, part, by], s2r[s, part, by])
            ubuf[s, part] = value
        whole, scale = coded(ubuf[s, 1 - h], 0)
        q3s[s] = whole
        s3s[s] = scale
        send(q3s.at[s], q3r.at[s], a3s.at[s], a3r.at[s], far)
        send(s3s.at[s], s3r.at[s], b3s.at[s], b3r.at[s], far)

    def final(s):
        arrived(q3s.at[s], q3r.at[s], a3s.at[s], a3r.at[s])
        arrived(s3s.at[s], s3r.at[s], b3s.at[s], b3r.at[s])
        return ubuf[s, h] + decoded(q3r[s], s3r[s])

    def prepare(s):
        @pl.loop(0, KPG)
        def _(k):
            widen(packed[s, k], c, k)

    def finish(s):
        arrived(packed.at[s], other.at[s], xs.at[s], xr.at[s])

        @pl.loop(0, KPG)
        def _(k):
            widen(other[s, k], 1 - c, k)
        multiply(s)

    prepare(0)
    mine.wait()
    arrived(left_hbm, left.at[1], xs.at[2], xr.at[2])
    finish(0)
    stage1_open(0)
    prepare(1)
    stage1_relay(0)
    finish(1)
    stage1_open(1)
    stage2(0)
    stage1_relay(1)
    stage3(0)
    stage2(1)
    first = final(0)
    stage3(1)
    second = final(1)
    for j in range(JB):
        out[:, j * BLK:(j + 1) * BLK] = jnp.concatenate(
            [first[:, j * WIDTH:(j + 1) * WIDTH], second[:, j * WIDTH:(j + 1) * WIDTH]], axis=1)
    for copy in started:
        copy.wait_send()


def local(left_blocks, left_cols, right_blocks, right_cols):
    r = lax.axis_index("row")
    c = lax.axis_index("col")
    d = lax.axis_index("depth")
    rows_idx = lax.dynamic_slice(left_cols, (c * ROWS, 0, d, 0), (ROWS, 2, 1, 2)).reshape(-1)
    by_layer = right_cols.reshape(2, 32, KPG, 2, 2)
    right_idx = lax.dynamic_slice(by_layer, (0, d, 0, r, 0), (2, 1, KPG, 1, 2)).reshape(-1)
    idx = jnp.concatenate([rows_idx, right_idx])
    dma = pltpu.SemaphoreType.DMA
    vmem = pltpu.VMEM
    q1 = vmem((PASSES, 2, 6, 2, HALF, NCOL), jnp.int16)
    s1 = vmem((PASSES, 2, 6, 1, NCOL), jnp.float32)
    q2 = vmem((PASSES, 2, 3, HALF, NCOL), jnp.int16)
    s2 = vmem((PASSES, 2, 3, 1, NCOL), jnp.float32)
    q3 = vmem((PASSES, HALF, NCOL), jnp.int16)
    s3 = vmem((PASSES, 1, NCOL), jnp.float32)
    n1, n2, n3 = PASSES * 12, PASSES * 6, PASSES
    return pl.pallas_call(
        kernel,
        out_shape=jax.ShapeDtypeStruct((HALF, JB * BLK), jnp.float32),
        in_specs=[
            pl.BlockSpec(memory_space=pltpu.SMEM),
            pl.BlockSpec(memory_space=pl.ANY),
            pl.BlockSpec(memory_space=pltpu.VMEM),
        ],
        out_specs=pl.BlockSpec(memory_space=pltpu.VMEM),
        scratch_shapes=[
            vmem((2, ROWS, 2, BLK, BLK), jnp.bfloat16),
            vmem((PASSES, KPG, BLK, BLK), jnp.bfloat16),
            vmem((PASSES, KPG, BLK, BLK), jnp.bfloat16),
            vmem((2 * KPG, BLK, NCOL), jnp.bfloat16),
            vmem((PASSES, 4, 4, BLK, NCOL), jnp.float32),
            vmem((PASSES, 2, HALF, NCOL), jnp.float32),
            q1, q1, s1, s1, q2, q2, s2, s2, q3, q3, s3, s3,
            dma, dma((3,)), dma((3,)),
            dma((n1,)), dma((n1,)), dma((n1,)), dma((n1,)),
            dma((n2,)), dma((n2,)), dma((n2,)), dma((n2,)),
            dma((n3,)), dma((n3,)), dma((n3,)), dma((n3,)),
        ],
        compiler_params=pltpu.CompilerParams(
            collective_id=0, has_side_effects=True, vmem_limit_bytes=48 << 20),
    )(idx, left_blocks.reshape(ROWS, 2, BLK, BLK), right_blocks.reshape(KPG, 2, BLK, BLK))


def solution(mesh):
    return jax.shard_map(
        local,
        mesh=mesh,
        in_specs=(
            P("col", "row", "depth", None, None, None),
            P(),
            P(("col", "depth"), "row", None, None, None),
            P(),
        ),
        out_specs=P(("col", "depth"), "row"),
        check_vma=False,
    )
```

time: 256 us -> 48.4 us (0.19)
  waiting for transfers between devices: 211 us -> 0 us
  Pallas kernels: 0 us -> 42.5 us
  local copies, waits for them, and re-layouts: 19.4 us -> 5.48 us
  between operations: 13.5 us -> 0.04 us
  matrix products: 7.41 us -> 0 us
  other arithmetic: 2.79 us -> 0.08 us
    reduce_scatter x1 -> x0, waiting for transfers between devices: 199 us -> none  [local(): lax.psum_scatter(flat_totals, 'depth', scatter_dimension=0, tiled=True)]
    pallas_call x0 -> x1, Pallas kernels: none -> 42.5 us  [local(): pl.pallas_call(kernel, out_shape=jax.ShapeDtypeStruct((HALF, JB * BLK), j...]
    gather x2 -> x0, local copies, waits for them, and re-layouts: 11.5 us -> none  [multiply(): picked = jnp.take(spread, a_cols, axis=0)]
    psum x1 -> x0, waiting for transfers between devices: 8.69 us -> none  [from_root(): return lax.psum(kept, axis)]
    dot_general x4 -> x0, matrix products: 7.41 us -> none  [the longest x2 4.99 us: multiply(): jnp.einsum('iaxy,ialyz->ixlz', left_panel, picked, preferred_element_type...]
    ppermute x1 -> x0, waiting for transfers between devices: 3.11 us -> none  [shifted(): lax.ppermute(value, axis, [(i, (i + by) % devices) for i in range(devices)])]
    select_n x2 -> x0, other arithmetic: 2.75 us -> none  [the longest x1 2.75 us: from_root(): jnp.where(lax.axis_index(axis) == source, value, 0).astype(value.dtype)]
    unnamed x11 -> x9, local copies, waits for them, and re-layouts: 6.14 us -> 4.35 us
  transfers between devices with their start and end apart: 3 -> 0, of which waited for: 3 -> 0; matrix products, arithmetic and copies ran while one was open for 6% -> 0% of each run, Pallas kernels for 0% -> 0%
where the time goes in v1:
time: 48.4 us; the launch traced here: 48.1 us
  Pallas kernels  42.5 us (88%)
  local copies, waits for them, and re-layouts  5.48 us (11%)
    pallas_call x1, Pallas kernels, local(): pl.pallas_call(kernel, out_shape=jax.ShapeDtypeStruct((HALF, JB * BLK), j...  42.5 us
    unnamed x9, local copies, waits for them, and re-layouts  4.35 us

profile of v1, /device:TPU:0, one launch (start us, length us, event | category | flops | bytes accessed | tf_op | source)
XLA Modules:
  0.0 48.1 jit_solution(11216810525965198913)
XLA Ops:
  0.0 0.0 copy-start
  0.0 0.8 %copy-done = s32[32,2,32,2]{2,3,1,0:T(2,128)S(1)} copy-done((s32[32,2,32,2]{2,3,1,0:T(2,128)S(1)}, s32[32,2,32,2]{2,3,1,0:T(2,128)}, u32[]{:S(2)}) %copy-start) | copy-done | bytes 16408
  0.8 0.7 %dynamic-slice_reduce_fusion = s32[16,2,2]{2,1,0:T(2,128)S(1)} fusion(s32[32,2,32,2]{2,3,1,0:T(2,128)S(1)} %copy-done, s32[]{:T(128)S(6)} %select_n.10, s32[]{:T(128)S(6)} %select_n.11), kind=kLoop, calls=%fused_computation | loop fusion | bytes 520 | tf_op jit(solution)/shard_map/dynamic_slice | solution.py:234
  1.6 0.0 copy-start.3
  1.6 0.1 reshape.15
  1.7 0.6 %copy-done.3 = s32[512,2,2]{0,2,1:T(2,128)S(1)} copy-done((s32[512,2,2]{0,2,1:T(2,128)S(1)}, s32[512,2,2]{0,2,1:T(2,128)}, u32[]{:S(2)}) %copy-start.3) | copy-done | bytes 8216
  2.3 0.1 reshape.16
  2.4 0.1 copy.6
  2.5 0.1 reshape.17
  2.6 0.1 pad_add_fusion.idx
  2.7 0.0 copy-start.1
  2.7 1.2 %copy-done.1 = bf16[16,1,1,2,128,128]{5,4,3,2,1,0:T(8,128)(2,1)S(1)} copy-done((bf16[16,1,1,2,128,128]{5,4,3,2,1,0:T(8,128)(2,1)S(1)}, bf16[16,1,1,2,128,128]{5,4,3,2,1,0:T(8,128)(2,1)}, u32[]{:S(2)}) %copy-start.1) | copy-done | bytes 1048600
  3.9 0.0 copy-start.2
  3.9 1.0 %copy-done.2 = bf16[8,1,2,128,128]{4,3,2,1,0:T(8,128)(2,1)S(1)} copy-done((bf16[8,1,2,128,128]{4,3,2,1,0:T(8,128)(2,1)S(1)}, bf16[8,1,2,128,128]{4,3,2,1,0:T(8,128)(2,1)}, u32[]{:S(2)}) %copy-start.2) | copy-done | bytes 524312
  4.9 42.5 %shard_map.46 = f32[64,512]{1,0:T(8,128)S(1)} custom-call(s32[96]{0:T(128)S(1)} %pad_add_fusion.idx, bf16[16,2,128,128]{3,2,1,0:T(8,128)(2,1)S(1)} %bitcast.8, bf16[8,2,128,128]{3,2,1,0:T(8,128)(2,1)S(1)} %bitcast.9), custom_call_target="tpu_custom_call" | custom-call | tf_op jit(solution)/shard_map/pallas_call | solution.py:247
  47.4 0.7 %copy.8 = f32[64,512]{1,0:T(8,128)} copy(f32[64,512]{1,0:T(8,128)S(1)} %shard_map.46) | data formatting | bytes 262144
  (1 shorter events, 0.0 us)
Async XLA Ops:
  0.0 0.8 %copy-start = (s32[32,2,32,2]{2,3,1,0:T(2,128)S(1)}, s32[32,2,32,2]{2,3,1,0:T(2,128)}, u32[]{:S(2)}) copy-start(s32[32,2,32,2]{2,3,1,0:T(2,128)} %param.5) | copy-start | bytes 49156
  1.6 0.7 %copy-start.3 = (s32[512,2,2]{0,2,1:T(2,128)S(1)}, s32[512,2,2]{0,2,1:T(2,128)}, u32[]{:S(2)}) copy-start(s32[512,2,2]{0,2,1:T(2,128)} %param.7) | copy-start | bytes 24580
  2.7 1.2 %copy-start.1 = (bf16[16,1,1,2,128,128]{5,4,3,2,1,0:T(8,128)(2,1)S(1)}, bf16[16,1,1,2,128,128]{5,4,3,2,1,0:T(8,128)(2,1)}, u32[]{:S(2)}) copy-start(bf16[16,1,1,2,128,128]{5,4,3,2,1,0:T(8,128)(2,1)} %param.4) | copy-start | bytes 3145732
  3.9 1.0 %copy-start.2 = (bf16[8,1,2,128,128]{4,3,2,1,0:T(8,128)(2,1)S(1)}, bf16[8,1,2,128,128]{4,3,2,1,0:T(8,128)(2,1)}, u32[]{:S(2)}) copy-start(bf16[8,1,2,128,128]{4,3,2,1,0:T(8,128)(2,1)} %param.6) | copy-start | bytes 1572868

commit v2 on v1

--- a/solution.py
+++ b/solution.py
@@ -27,9 +27,9 @@
     return whole.astype(jnp.int32).astype(jnp.float32) * scale
 
 
-def kernel(idx, left_hbm, right, out, left, packed, other, spread, acc, ubuf,
+def kernel(lcols_hbm, rcols_hbm, left_hbm, right_hbm, out, lcols, rcols, right, left, packed, other, spread, acc, ubuf,
            q1s, q1r, s1s, s1r, q2s, q2r, s2s, s2r, q3s, q3r, s3s, s3r,
-           lsem, xs, xr, a1s, a1r, b1s, b1r, a2s, a2r, b2s, b2r, a3s, a3r, b3s, b3r):
+           lsem, isem, xs, xr, a1s, a1r, b1s, b1r, a2s, a2r, b2s, b2r, a3s, a3r, b3s, b3r):
     r = lax.axis_index("row")
     c = lax.axis_index("col")
     d = lax.axis_index("depth")
@@ -43,6 +43,15 @@
         lambda by: at(z + by, y, h),
         lambda by: at(z, y + by, h),
     )
+    mine = pltpu.make_async_copy(left_hbm, left.at[0], lsem.at[0])
+    margin = pltpu.make_async_copy(right_hbm, right, lsem.at[1])
+    left_index = pltpu.make_async_copy(lcols_hbm.at[pl.ds(c * ROWS, ROWS)], lcols, isem.at[0])
+    right_index = pltpu.make_async_copy(rcols_hbm, rcols, isem.at[1])
+    margin.start()
+    mine.start()
+    left_index.start()
+    right_index.start()
+
     barrier = pltpu.get_barrier_semaphore()
     peers = [mate, peer, far] + [go(by) for go in along for by in (1, 2, 3)]
     for device in peers:
@@ -62,11 +71,7 @@
             src_ref=src, dst_ref=dst, send_sem=ssem, recv_sem=rsem,
             device_id=mate, device_id_type=MESH).wait_recv()
 
-    mine = pltpu.make_async_copy(left_hbm, left.at[0], lsem)
-    mine.start()
-
-    low = lax.broadcasted_iota(jnp.int32, (BLK, BLK), 1) < HALF
-
+    margin.wait()
     for k in range(KPG):
         one, two = right[k, 0], right[k, 1]
         packed[0, k] = jnp.concatenate([one[:, :HALF], two[:, :HALF]], axis=1)
@@ -81,8 +86,8 @@
     upper = (lane >= HALF).astype(jnp.int32)
 
     def widen(block, group, k):
-        base = ROWS * 4 + (group * KPG + k) * 2
-        j0, j1 = idx[base], idx[base + 1]
+        row = group * (32 * KPG) + d * KPG + k
+        j0, j1 = rcols[r, 0, row], rcols[r, 1, row]
         turned = pltpu.roll(block, HALF, 1)
         straight = jnp.where(upper == 0, j0, j1)
         crossed = jnp.where(upper == 0, j1, j0)
@@ -92,20 +97,20 @@
             swap = (crossed == target).astype(jnp.float32).astype(jnp.bfloat16)
             spread[group * KPG + k, :, t * BLK:(t + 1) * BLK] = block * keep + turned * swap
 
-    def multiply(s):
+    def multiply(s, group, add):
+        slot = (group + r) % 2
+
         @pl.loop(0, ROWS // 4)
         def _(block_z):
             for block_y in range(4):
                 i = block_z * 4 + block_y
-                total = None
-                for slot, group in ((0, r), (1, 1 - r)):
-                    base = (i * 2 + group) * 2
-                    a0, a1 = idx[base], idx[base + 1]
-                    lhs = jnp.concatenate([left[slot, i, 0], left[slot, i, 1]], axis=1)
-                    rhs = jnp.concatenate([spread[group * KPG + a0], spread[group * KPG + a1]], axis=0)
-                    term = jnp.dot(lhs, rhs, preferred_element_type=jnp.float32)
-                    total = term if total is None else total + term
-                acc[s, block_z, block_y] = total
+                a0, a1 = lcols[i, group, 0, d], lcols[i, group, 1, d]
+                lhs = jnp.concatenate([left[slot, i, 0], left[slot, i, 1]], axis=1)
+                rhs = jnp.concatenate([spread[group * KPG + a0], spread[group * KPG + a1]], axis=0)
+                term = jnp.dot(lhs, rhs, preferred_element_type=jnp.float32)
+                if add:
+                    term = term + acc[s, block_z, block_y]
+                acc[s, block_z, block_y] = term
 
     where = (z, y)
 
@@ -191,10 +196,11 @@
         arrived(s3s.at[s], s3r.at[s], b3s.at[s], b3r.at[s])
         return ubuf[s, h] + decoded(q3r[s], s3r[s])
 
-    def prepare(s):
+    def begin(s):
         @pl.loop(0, KPG)
         def _(k):
             widen(packed[s, k], c, k)
+        multiply(s, c, False)
 
     def finish(s):
         arrived(packed.at[s], other.at[s], xs.at[s], xr.at[s])
@@ -202,14 +208,16 @@
         @pl.loop(0, KPG)
         def _(k):
             widen(other[s, k], 1 - c, k)
-        multiply(s)
-
-    prepare(0)
+        multiply(s, 1 - c, True)
+
+    left_index.wait()
+    right_index.wait()
     mine.wait()
     arrived(left_hbm, left.at[1], xs.at[2], xr.at[2])
+    begin(0)
+    begin(1)
     finish(0)
     stage1_open(0)
-    prepare(1)
     stage1_relay(0)
     finish(1)
     stage1_open(1)
@@ -228,13 +236,6 @@
 
 
 def local(left_blocks, left_cols, right_blocks, right_cols):
-    r = lax.axis_index("row")
-    c = lax.axis_index("col")
-    d = lax.axis_index("depth")
-    rows_idx = lax.dynamic_slice(left_cols, (c * ROWS, 0, d, 0), (ROWS, 2, 1, 2)).reshape(-1)
-    by_layer = right_cols.reshape(2, 32, KPG, 2, 2)
-    right_idx = lax.dynamic_slice(by_layer, (0, d, 0, r, 0), (2, 1, KPG, 1, 2)).reshape(-1)
-    idx = jnp.concatenate([rows_idx, right_idx])
     dma = pltpu.SemaphoreType.DMA
     vmem = pltpu.VMEM
     q1 = vmem((PASSES, 2, 6, 2, HALF, NCOL), jnp.int16)
@@ -247,13 +248,12 @@
     return pl.pallas_call(
         kernel,
         out_shape=jax.ShapeDtypeStruct((HALF, JB * BLK), jnp.float32),
-        in_specs=[
-            pl.BlockSpec(memory_space=pltpu.SMEM),
-            pl.BlockSpec(memory_space=pl.ANY),
-            pl.BlockSpec(memory_space=pltpu.VMEM),
-        ],
+        in_specs=[pl.BlockSpec(memory_space=pl.ANY)] * 4,
         out_specs=pl.BlockSpec(memory_space=pltpu.VMEM),
         scratch_shapes=[
+            pltpu.SMEM((ROWS, 2, 2, 32), jnp.int32),
+            pltpu.SMEM((2, 2, 2 * 32 * KPG), jnp.int32),
+            vmem((KPG, 2, BLK, BLK), jnp.bfloat16),
             vmem((2, ROWS, 2, BLK, BLK), jnp.bfloat16),
             vmem((PASSES, KPG, BLK, BLK), jnp.bfloat16),
             vmem((PASSES, KPG, BLK, BLK), jnp.bfloat16),
@@ -261,14 +261,14 @@
             vmem((PASSES, 4, 4, BLK, NCOL), jnp.float32),
             vmem((PASSES, 2, HALF, NCOL), jnp.float32),
             q1, q1, s1, s1, q2, q2, s2, s2, q3, q3, s3, s3,
-            dma, dma((3,)), dma((3,)),
+            dma((2,)), dma((2,)), dma((3,)), dma((3,)),
             dma((n1,)), dma((n1,)), dma((n1,)), dma((n1,)),
             dma((n2,)), dma((n2,)), dma((n2,)), dma((n2,)),
             dma((n3,)), dma((n3,)), dma((n3,)), dma((n3,)),
         ],
         compiler_params=pltpu.CompilerParams(
-            collective_id=0, has_side_effects=True, vmem_limit_bytes=48 << 20),
-    )(idx, left_blocks.reshape(ROWS, 2, BLK, BLK), right_blocks.reshape(KPG, 2, BLK, BLK))
+            collective_id=0, has_side_effects=True, vmem_limit_bytes=67_043_328),
+    )(left_cols.transpose(0, 1, 3, 2), right_cols.transpose(1, 2, 0), left_blocks.reshape(ROWS, 2, BLK, BLK), right_blocks.reshape(KPG, 2, BLK, BLK))
 
 
 def solution(mesh):

time: 48.4 us -> 43.6 us (0.901)
  local copies, waits for them, and re-layouts: 5.48 us -> 1.57 us
  Pallas kernels: 42.5 us -> 41.9 us
    unnamed x9 -> x1, local copies, waits for them, and re-layouts: 4.35 us -> 1.57 us
    dynamic_slice x3 -> x0, local copies, waits for them, and re-layouts: 0.83 us -> none  [the longest x1 0.73 us: local(): lax.dynamic_slice(left_cols, (c * ROWS, 0, d, 0), (ROWS, 2, 1, 2))]
    pallas_call x1, Pallas kernels: 42.5 us -> 41.9 us  [local(): pl.pallas_call(kernel, out_shape=jax.ShapeDtypeStruct((HALF, JB * BLK), j...]
where the time goes in v2:
time: 43.6 us; the launch traced here: 43.4 us
  Pallas kernels  41.9 us (96%)
  local copies, waits for them, and re-layouts  1.57 us (4%)
    pallas_call x1, Pallas kernels, local(): pl.pallas_call(kernel, out_shape=jax.ShapeDtypeStruct((HALF, JB * BLK), j...  41.9 us
    unnamed x1, local copies, waits for them, and re-layouts  1.57 us

profile of v2, /device:TPU:0, one launch (start us, length us, event | category | flops | bytes accessed | tf_op | source)
XLA Modules:
  0.0 43.4 jit_solution(5405061869161876286)
XLA Ops:
  0.0 41.9 %shard_map.46 = f32[64,512]{1,0:T(8,128)} custom-call(s32[32,2,2,32]{3,2,1,0:T(2,128)} %bitcast.6, s32[2,2,512]{2,1,0:T(2,128)} %bitcast.7, bf16[16,2,128,128]{3,2,1,0:T(8,128)(2,1)} %bitcast.4, bf16[8,2,128,128]{3,2,1,0:T(8,128)(2,1)} %bitcast.5), custom_call_target="tpu_custom_call" | custom-call | tf_op jit(solution)/shard_map/pallas_call | solution.py:248
  41.9 1.6 %copy.6 = f32[64,512]{1,0:T(8,128)} copy(f32[64,512]{1,0:T(8,128)} %shard_map.46) | data formatting | bytes 262144

commit v3 on v2

--- a/solution.py
+++ b/solution.py
@@ -7,7 +7,7 @@
 
 BLK = 128
 JB = 4
-PASSES = 2
+PASSES = 4
 WIDTH = BLK // PASSES
 NCOL = JB * WIDTH
 ROWS = 16
@@ -72,30 +72,31 @@
             device_id=mate, device_id_type=MESH).wait_recv()
 
     margin.wait()
-    for k in range(KPG):
-        one, two = right[k, 0], right[k, 1]
-        packed[0, k] = jnp.concatenate([one[:, :HALF], two[:, :HALF]], axis=1)
-        packed[1, k] = jnp.concatenate([one[:, HALF:], two[:, HALF:]], axis=1)
+    for k in range(0, KPG, 2):
+        blocks = [right[k, 0], right[k, 1], right[k + 1, 0], right[k + 1, 1]]
+        for s in range(PASSES):
+            packed[s, k // 2] = jnp.concatenate([b[:, s * WIDTH:(s + 1) * WIDTH] for b in blocks], axis=1)
 
     pl.semaphore_wait(barrier, len(peers))
     for s in range(PASSES):
         send(packed.at[s], other.at[s], xs.at[s], xr.at[s], peer)
-    send(left_hbm, left.at[1], xs.at[2], xr.at[2], mate)
-
-    lane = lax.broadcasted_iota(jnp.int32, (1, BLK), 1)
-    upper = (lane >= HALF).astype(jnp.int32)
-
-    def widen(block, group, k):
-        row = group * (32 * KPG) + d * KPG + k
-        j0, j1 = rcols[r, 0, row], rcols[r, 1, row]
-        turned = pltpu.roll(block, HALF, 1)
-        straight = jnp.where(upper == 0, j0, j1)
-        crossed = jnp.where(upper == 0, j1, j0)
-        for t in range(2):
-            target = upper + 2 * t
-            keep = (straight == target).astype(jnp.float32).astype(jnp.bfloat16)
-            swap = (crossed == target).astype(jnp.float32).astype(jnp.bfloat16)
-            spread[group * KPG + k, :, t * BLK:(t + 1) * BLK] = block * keep + turned * swap
+    send(left_hbm, left.at[1], xs.at[PASSES], xr.at[PASSES], mate)
+
+    target = lax.broadcasted_iota(jnp.int32, (1, BLK), 1) // WIDTH
+
+    def widen(two_rows, group, pair):
+        turned = [two_rows] + [pltpu.roll(two_rows, by * WIDTH, 1) for by in range(1, JB)]
+        for odd in range(2):
+            k = 2 * pair + odd
+            row = group * (32 * KPG) + d * KPG + k
+            j0, j1 = rcols[r, 0, row], rcols[r, 1, row]
+            turn = jnp.where(target == j0, (target - 2 * odd) & 3,
+                             jnp.where(target == j1, (target - 2 * odd - 1) & 3, -1))
+            total = None
+            for by in range(JB):
+                term = turned[by] * (turn == by).astype(jnp.float32).astype(jnp.bfloat16)
+                total = term if total is None else total + term
+            spread[group * KPG + k] = total
 
     def multiply(s, group, add):
         slot = (group + r) % 2
@@ -197,40 +198,41 @@
         return ubuf[s, h] + decoded(q3r[s], s3r[s])
 
     def begin(s):
-        @pl.loop(0, KPG)
-        def _(k):
-            widen(packed[s, k], c, k)
+        @pl.loop(0, KPG // 2)
+        def _(pair):
+            widen(packed[s, pair], c, pair)
         multiply(s, c, False)
 
     def finish(s):
         arrived(packed.at[s], other.at[s], xs.at[s], xr.at[s])
 
-        @pl.loop(0, KPG)
-        def _(k):
-            widen(other[s, k], 1 - c, k)
+        @pl.loop(0, KPG // 2)
+        def _(pair):
+            widen(other[s, pair], 1 - c, pair)
         multiply(s, 1 - c, True)
 
     left_index.wait()
     right_index.wait()
     mine.wait()
-    arrived(left_hbm, left.at[1], xs.at[2], xr.at[2])
-    begin(0)
-    begin(1)
-    finish(0)
-    stage1_open(0)
-    stage1_relay(0)
-    finish(1)
-    stage1_open(1)
-    stage2(0)
-    stage1_relay(1)
-    stage3(0)
-    stage2(1)
-    first = final(0)
-    stage3(1)
-    second = final(1)
+    arrived(left_hbm, left.at[1], xs.at[PASSES], xr.at[PASSES])
+    for s in range(PASSES):
+        begin(s)
+    ready = []
+    for step in range(PASSES + 4):
+        if step < PASSES:
+            finish(step)
+            stage1_open(step)
+        if 0 <= step - 1 < PASSES:
+            stage1_relay(step - 1)
+        if 0 <= step - 2 < PASSES:
+            stage2(step - 2)
+        if 0 <= step - 3 < PASSES:
+            stage3(step - 3)
+        if 0 <= step - 4 < PASSES:
+            ready.append(final(step - 4))
     for j in range(JB):
         out[:, j * BLK:(j + 1) * BLK] = jnp.concatenate(
-            [first[:, j * WIDTH:(j + 1) * WIDTH], second[:, j * WIDTH:(j + 1) * WIDTH]], axis=1)
+            [one[:, j * WIDTH:(j + 1) * WIDTH] for one in ready], axis=1)
     for copy in started:
         copy.wait_send()
 
@@ -255,13 +257,13 @@
             pltpu.SMEM((2, 2, 2 * 32 * KPG), jnp.int32),
             vmem((KPG, 2, BLK, BLK), jnp.bfloat16),
             vmem((2, ROWS, 2, BLK, BLK), jnp.bfloat16),
-            vmem((PASSES, KPG, BLK, BLK), jnp.bfloat16),
-            vmem((PASSES, KPG, BLK, BLK), jnp.bfloat16),
+            vmem((PASSES, KPG // 2, BLK, BLK), jnp.bfloat16),
+            vmem((PASSES, KPG // 2, BLK, BLK), jnp.bfloat16),
             vmem((2 * KPG, BLK, NCOL), jnp.bfloat16),
             vmem((PASSES, 4, 4, BLK, NCOL), jnp.float32),
             vmem((PASSES, 2, HALF, NCOL), jnp.float32),
             q1, q1, s1, s1, q2, q2, s2, s2, q3, q3, s3, s3,
-            dma((2,)), dma((2,)), dma((3,)), dma((3,)),
+            dma((2,)), dma((2,)), dma((PASSES + 1,)), dma((PASSES + 1,)),
             dma((n1,)), dma((n1,)), dma((n1,)), dma((n1,)),
             dma((n2,)), dma((n2,)), dma((n2,)), dma((n2,)),
             dma((n3,)), dma((n3,)), dma((n3,)), dma((n3,)),

time: 43.6 us -> 45.2 us (1.037)
  Pallas kernels: 41.9 us -> 43.5 us
    pallas_call x1, Pallas kernels: 41.9 us -> 43.5 us  [local(): pl.pallas_call(kernel, out_shape=jax.ShapeDtypeStruct((HALF, JB * BLK), j...]
where the time goes in v3:
time: 45.2 us; the launch traced here: 45.1 us
  Pallas kernels  43.5 us (96%)
  local copies, waits for them, and re-layouts  1.57 us (3%)
    pallas_call x1, Pallas kernels, local(): pl.pallas_call(kernel, out_shape=jax.ShapeDtypeStruct((HALF, JB * BLK), j...  43.5 us
    unnamed x1, local copies, waits for them, and re-layouts  1.57 us

profile of v3, /device:TPU:0, one launch (start us, length us, event | category | flops | bytes accessed | tf_op | source)
XLA Modules:
  0.0 45.1 jit_solution(13044696081634513087)
XLA Ops:
  0.0 43.5 %shard_map.46 = f32[64,512]{1,0:T(8,128)} custom-call(s32[32,2,2,32]{3,2,1,0:T(2,128)} %bitcast.6, s32[2,2,512]{2,1,0:T(2,128)} %bitcast.7, bf16[16,2,128,128]{3,2,1,0:T(8,128)(2,1)} %bitcast.4, bf16[8,2,128,128]{3,2,1,0:T(8,128)(2,1)} %bitcast.5), custom_call_target="tpu_custom_call" | custom-call | tf_op jit(solution)/shard_map/pallas_call | solution.py:250
  43.5 1.6 %copy.6 = f32[64,512]{1,0:T(8,128)} copy(f32[64,512]{1,0:T(8,128)} %shard_map.46) | data formatting | bytes 262144

commit v4 on v2

--- a/solution.py
+++ b/solution.py
@@ -137,34 +137,22 @@
         arrived(q1s.at[s, part, slot], q1r.at[s, part, slot], a1s.at[n], a1r.at[n])
         arrived(s1s.at[s, part, slot], s1r.at[s, part, slot], b1s.at[n], b1r.at[n])
 
-    def stage1_open(s):
-        for part in range(2):
-            v = where[part]
-            post1(s, part, 0, own(s, part, 0, (v + 2) % 4), 1)
-            post1(s, part, 1, own(s, part, 1, (v + 2) % 4), 3)
-        for part in range(2):
-            v = where[part]
-            post1(s, part, 3, own(s, part, 1, (v + 1) % 4), 1)
-            post1(s, part, 4, own(s, part, 0, (v + 3) % 4), 3)
-
-    def stage1_relay(s):
-        for part in range(2):
-            v = where[part]
-            for slot, pair, by in ((0, 0, 1), (1, 1, 3)):
-                got1(s, part, slot)
-                value = own(s, part, pair, (v + by) % 4) + decoded(q1r[s, part, slot], s1r[s, part, slot])
-                post1(s, part, 2 if slot == 0 else 5, value, by)
+    def stage1(s):
+        for by in (2, 1, 3):
+            for part in range(2):
+                for pair in range(2):
+                    post1(s, part, 2 * (by - 1) + pair, own(s, part, pair, (where[part] + by) % 4), by)
 
     def reduced(s, part, w):
         value = one(s, part, w, where[part])
-        for first in (2, 4):
+        for first in (0, 2, 4):
             pair = first + w // 2
             value = value + decoded(q1r[s, part, pair, w % 2], s1r[s, part, pair])
         return value
 
     def stage2(s):
         for part in range(2):
-            for slot in (3, 4, 2, 5):
+            for slot in (4, 5, 0, 1, 2, 3):
                 got1(s, part, slot)
             v = where[1 - part]
             for by in (2, 1, 3):
@@ -217,12 +205,10 @@
     begin(0)
     begin(1)
     finish(0)
-    stage1_open(0)
-    stage1_relay(0)
+    stage1(0)
     finish(1)
-    stage1_open(1)
+    stage1(1)
     stage2(0)
-    stage1_relay(1)
     stage3(0)
     stage2(1)
     first = final(0)

time: 43.6 us -> 42.2 us (0.968)
  Pallas kernels: 41.9 us -> 40.5 us
    pallas_call x1, Pallas kernels: 41.9 us -> 40.5 us  [local(): pl.pallas_call(kernel, out_shape=jax.ShapeDtypeStruct((HALF, JB * BLK), j...]
where the time goes in v4:
time: 42.2 us; the launch traced here: 42.1 us
  Pallas kernels  40.5 us (96%)
  local copies, waits for them, and re-layouts  1.57 us (4%)
    pallas_call x1, Pallas kernels, local(): pl.pallas_call(kernel, out_shape=jax.ShapeDtypeStruct((HALF, JB * BLK), j...  40.5 us
    unnamed x1, local copies, waits for them, and re-layouts  1.57 us

profile of v4, /device:TPU:0, one launch (start us, length us, event | category | flops | bytes accessed | tf_op | source)
XLA Modules:
  0.0 42.1 jit_solution(6423738110868723509)
XLA Ops:
  0.0 40.5 %shard_map.46 = f32[64,512]{1,0:T(8,128)} custom-call(s32[32,2,2,32]{3,2,1,0:T(2,128)} %bitcast.6, s32[2,2,512]{2,1,0:T(2,128)} %bitcast.7, bf16[16,2,128,128]{3,2,1,0:T(8,128)(2,1)} %bitcast.4, bf16[8,2,128,128]{3,2,1,0:T(8,128)(2,1)} %bitcast.5), custom_call_target="tpu_custom_call" | custom-call | tf_op jit(solution)/shard_map/pallas_call | solution.py:234
  40.5 1.6 %copy.6 = f32[64,512]{1,0:T(8,128)} copy(f32[64,512]{1,0:T(8,128)} %shard_map.46) | data formatting | bytes 262144

commit v5 on v4

--- a/solution.py
+++ b/solution.py
@@ -28,8 +28,8 @@
 
 
 def kernel(lcols_hbm, rcols_hbm, left_hbm, right_hbm, out, lcols, rcols, right, left, packed, other, spread, acc, ubuf,
-           q1s, q1r, s1s, s1r, q2s, q2r, s2s, s2r, q3s, q3r, s3s, s3r,
-           lsem, isem, xs, xr, a1s, a1r, b1s, b1r, a2s, a2r, b2s, b2r, a3s, a3r, b3s, b3r):
+           q1s, q1r, s1s, s1r, q2s, q2r, s2s, s2r,
+           lsem, isem, xs, xr, a1s, a1r, b1s, b1r, a2s, a2r, b2s, b2r):
     r = lax.axis_index("row")
     c = lax.axis_index("col")
     d = lax.axis_index("depth")
@@ -54,6 +54,7 @@
 
     barrier = pltpu.get_barrier_semaphore()
     peers = [mate, peer, far] + [go(by) for go in along for by in (1, 2, 3)]
+    peers += [at(z + by, y, 1 - h) for by in (1, 2, 3)] + [at(z, y + by, 1 - h) for by in (1, 2, 3)]
     for device in peers:
         pl.semaphore_signal(barrier, inc=1, device_id=device, device_id_type=MESH)
 
@@ -155,34 +156,29 @@
             for slot in (4, 5, 0, 1, 2, 3):
                 got1(s, part, slot)
             v = where[1 - part]
-            for by in (2, 1, 3):
-                whole, scale = coded(reduced(s, part, (v + by) % 4), 0)
-                q2s[s, part, by - 1] = whole
-                s2s[s, part, by - 1] = scale
-                n = (s * 2 + part) * 3 + by - 1
-                send(q2s.at[s, part, by - 1], q2r.at[s, part, by - 1], a2s.at[n], a2r.at[n], along[1 - part](by))
-                send(s2s.at[s, part, by - 1], s2r.at[s, part, by - 1], b2s.at[n], b2r.at[n], along[1 - part](by))
-            ubuf[s, part] = reduced(s, part, v)
-
-    def stage3(s):
-        for part in range(2):
-            value = ubuf[s, part]
-            for by in range(3):
-                n = (s * 2 + part) * 3 + by
-                arrived(q2s.at[s, part, by], q2r.at[s, part, by], a2s.at[n], a2r.at[n])
-                arrived(s2s.at[s, part, by], s2r.at[s, part, by], b2s.at[n], b2r.at[n])
-                value = value + decoded(q2r[s, part, by], s2r[s, part, by])
-            ubuf[s, part] = value
-        whole, scale = coded(ubuf[s, 1 - h], 0)
-        q3s[s] = whole
-        s3s[s] = scale
-        send(q3s.at[s], q3r.at[s], a3s.at[s], a3r.at[s], far)
-        send(s3s.at[s], s3r.at[s], b3s.at[s], b3r.at[s], far)
+            for by in (2, 1, 3, 0):
+                value = reduced(s, part, (v + by) % 4)
+                whole, scale = coded(value, 0)
+                q2s[s, part, by] = whole
+                s2s[s, part, by] = scale
+                if by == 0:
+                    ubuf[s, part] = value
+        for part, first in ((1 - h, 4), (h, 0)):
+            for by in (2, 1, 3, 0):
+                if first + by:
+                    n = s * 8 + first + by
+                    device = at(z + by * part, y + by * (1 - part), part)
+                    send(q2s.at[s, part, by], q2r.at[s, first + by], a2s.at[n], a2r.at[n], device)
+                    send(s2s.at[s, part, by], s2r.at[s, first + by], b2s.at[n], b2r.at[n], device)
 
     def final(s):
-        arrived(q3s.at[s], q3r.at[s], a3s.at[s], a3r.at[s])
-        arrived(s3s.at[s], s3r.at[s], b3s.at[s], b3r.at[s])
-        return ubuf[s, h] + decoded(q3r[s], s3r[s])
+        value = ubuf[s, h]
+        for slot in (1, 3, 2, 4, 5, 7, 6):
+            n = s * 8 + slot
+            arrived(q2r.at[s, slot], q2r.at[s, slot], a2s.at[n], a2r.at[n])
+            arrived(s2r.at[s, slot], s2r.at[s, slot], b2s.at[n], b2r.at[n])
+            value = value + decoded(q2r[s, slot], s2r[s, slot])
+        return value
 
     def begin(s):
         @pl.loop(0, KPG)
@@ -209,10 +205,8 @@
     finish(1)
     stage1(1)
     stage2(0)
-    stage3(0)
     stage2(1)
     first = final(0)
-    stage3(1)
     second = final(1)
     for j in range(JB):
         out[:, j * BLK:(j + 1) * BLK] = jnp.concatenate(
@@ -226,11 +220,11 @@
     vmem = pltpu.VMEM
     q1 = vmem((PASSES, 2, 6, 2, HALF, NCOL), jnp.int16)
     s1 = vmem((PASSES, 2, 6, 1, NCOL), jnp.float32)
-    q2 = vmem((PASSES, 2, 3, HALF, NCOL), jnp.int16)
-    s2 = vmem((PASSES, 2, 3, 1, NCOL), jnp.float32)
-    q3 = vmem((PASSES, HALF, NCOL), jnp.int16)
-    s3 = vmem((PASSES, 1, NCOL), jnp.float32)
-    n1, n2, n3 = PASSES * 12, PASSES * 6, PASSES
+    q2s = vmem((PASSES, 2, 4, HALF, NCOL), jnp.int16)
+    s2s = vmem((PASSES, 2, 4, 1, NCOL), jnp.float32)
+    q2r = vmem((PASSES, 8, HALF, NCOL), jnp.int16)
+    s2r = vmem((PASSES, 8, 1, NCOL), jnp.float32)
+    n1, n2 = PASSES * 12, PASSES * 8
     return pl.pallas_call(
         kernel,
         out_shape=jax.ShapeDtypeStruct((HALF, JB * BLK), jnp.float32),
@@ -246,11 +240,10 @@
             vmem((2 * KPG, BLK, NCOL), jnp.bfloat16),
             vmem((PASSES, 4, 4, BLK, NCOL), jnp.float32),
             vmem((PASSES, 2, HALF, NCOL), jnp.float32),
-            q1, q1, s1, s1, q2, q2, s2, s2, q3, q3, s3, s3,
+            q1, q1, s1, s1, q2s, q2r, s2s, s2r,
             dma((2,)), dma((2,)), dma((3,)), dma((3,)),
             dma((n1,)), dma((n1,)), dma((n1,)), dma((n1,)),
             dma((n2,)), dma((n2,)), dma((n2,)), dma((n2,)),
-            dma((n3,)), dma((n3,)), dma((n3,)), dma((n3,)),
         ],
         compiler_params=pltpu.CompilerParams(
             collective_id=0, has_side_effects=True, vmem_limit_bytes=67_043_328),

time: 42.2 us -> 40.9 us (0.969)
  Pallas kernels: 40.5 us -> 39.1 us
    pallas_call x1, Pallas kernels: 40.5 us -> 39.1 us  [local(): pl.pallas_call(kernel, out_shape=jax.ShapeDtypeStruct((HALF, JB * BLK), j...]
where the time goes in v5:
time: 40.9 us; the launch traced here: 40.7 us
  Pallas kernels  39.1 us (96%)
  local copies, waits for them, and re-layouts  1.57 us (4%)
    pallas_call x1, Pallas kernels, local(): pl.pallas_call(kernel, out_shape=jax.ShapeDtypeStruct((HALF, JB * BLK), j...  39.1 us
    unnamed x1, local copies, waits for them, and re-layouts  1.57 us

profile of v5, /device:TPU:0, one launch (start us, length us, event | category | flops | bytes accessed | tf_op | source)
XLA Modules:
  0.0 40.7 jit_solution(18023732225284757362)
XLA Ops:
  0.0 39.1 %shard_map.46 = f32[64,512]{1,0:T(8,128)} custom-call(s32[32,2,2,32]{3,2,1,0:T(2,128)} %bitcast.6, s32[2,2,512]{2,1,0:T(2,128)} %bitcast.7, bf16[16,2,128,128]{3,2,1,0:T(8,128)(2,1)} %bitcast.4, bf16[8,2,128,128]{3,2,1,0:T(8,128)(2,1)} %bitcast.5), custom_call_target="tpu_custom_call" | custom-call | tf_op jit(solution)/shard_map/pallas_call | solution.py:228
  39.1 1.6 %copy.6 = f32[64,512]{1,0:T(8,128)} copy(f32[64,512]{1,0:T(8,128)} %shard_map.46) | data formatting | bytes 262144
